TPU v7x, 32 devices: a whole 2x2x4 slice. The times are simulated.
32 devices in a mesh: blk: 4 (over x, core), shard: 8 (over z, y).
Axes of the slice: x: 2, y: 2, z: 4, core: 2. Of those that a mesh axis runs over, the one named last changes fastest.
Arguments:
- item_features: bfloat16 [32768, 1024], P('shard'), may hold values from -6 to 6
- tower_weight: bfloat16 [1024, 512], replicated, may hold values from -0.1875 to 0.1875
- gate_in: bfloat16 [64, 128], replicated, may hold values from -0.75 to 0.75
- gate_in_bias: bfloat16 [128], replicated, may hold values from -4 to 4
- gate_out: bfloat16 [128, 64], replicated, may hold values from -0.5 to 0.5
- gate_out_bias: bfloat16 [64], replicated, may hold values from -4 to 4
- user_table: bfloat16 [4096, 512], P(('blk', 'shard')), may hold values from -6 to 6
- user_ids: int32 [128], P(('blk', 'shard')), may hold values from 0 to 127
- positive_item: int32 [128, 16], P(('blk', 'shard')), may hold values from 0 to 2047
- listed_owner: int32 [128, 1], P(('blk', 'shard')), may hold values from 0 to 7; in each aligned block of 4 rows (0 to 3, 4 to 7, ...) at most 2 rows name the same one
- listed_slot: int32 [128], P(('blk', 'shard')), may hold values from 0 to 31
Outputs:
- tower_gradient: float32 [1024, 512], P('shard')
- user_gradient: float32 [4096, 512], P(('blk', 'shard'))
Inputs may be any that keep to these rules, and one draw needn't show every extreme that they name: `listed_owner`: at most 2 of the 4 listings of one trainer name the same owner. `user_ids`: A row of the trainer's own 128 rows of user_table. `positive_item`: A position among the rows of the user's circle.
All inputs are finite; a program needn't handle non-finite values.
Results may differ from a plain program's by a relative error of at most 0.0055.
Values may be sent and summed in bfloat16 or wider, within the bound.
A program may use at most 128 MiB of HBM per device.

v0:
```python
import math
import jax
import jax.numpy as jnp
from jax import lax
from jax.sharding import PartitionSpec as P

K = 8
H = 64
BLK = 128
CAP = 2
OWN = 32
USERS = 4
UTAB = 128
E = 512


def pair_terms(user_rows, item_rows, targets, gate_in, gate_in_bias, gate_out, gate_out_bias):
    count_users = user_rows.shape[0]
    count_items = item_rows.shape[0]
    scaling = 1.0 / math.sqrt(H)
    user_parts = user_rows.reshape(count_users * K, H)
    item_parts = item_rows.reshape(count_items, K, H)
    logits = (
        jnp.einsum("xh,ibh->xbi", user_parts, item_parts, preferred_element_type=jnp.float32)
        * scaling
    )
    logits = logits.reshape(count_users, K * K, count_items)
    gate_input = logits.astype(jnp.bfloat16)
    hidden_pre = jnp.einsum("pg,upi->ugi", gate_in, gate_input, preferred_element_type=jnp.float32)
    hidden_pre = hidden_pre + gate_in_bias.astype(jnp.float32)[None, :, None]
    hidden = jax.nn.silu(hidden_pre).astype(jnp.bfloat16)
    gate_logit = jnp.einsum("gp,ugi->upi", gate_out, hidden, preferred_element_type=jnp.float32)
    gate_logit = gate_logit + gate_out_bias.astype(jnp.float32)[None, :, None]
    exp_terms = jnp.exp(gate_logit)
    mixture = exp_terms / jnp.sum(exp_terms, axis=1, keepdims=True)
    scores = jnp.sum(mixture * logits, axis=1)
    score_grad = jax.nn.sigmoid(scores) - targets
    weighted = score_grad[:, None, :] * mixture
    logit_grad = (weighted * (logits - scores[:, None, :])).astype(jnp.bfloat16)
    gate_sig = jax.nn.sigmoid(hidden_pre)
    hidden_grad = jnp.einsum(
        "gp,upi->ugi", gate_out, logit_grad, preferred_element_type=jnp.float32
    )
    hidden_grad = (hidden_grad * gate_sig * (1.0 + hidden_pre * (1.0 - gate_sig))).astype(
        jnp.bfloat16
    )
    pair_grad = weighted + jnp.einsum(
        "pg,ugi->upi", gate_in, hidden_grad, preferred_element_type=jnp.float32
    )
    pair_grad = pair_grad.astype(jnp.bfloat16).reshape(count_users * K, K, count_items)
    user_delta = jnp.einsum(
        "xbi,ibh->xh", pair_grad, item_parts, preferred_element_type=jnp.float32
    )
    item_delta = jnp.einsum(
        "xbi,xh->ibh", pair_grad, user_parts, preferred_element_type=jnp.float32
    )
    return (
        user_delta.reshape(count_users, K * H) * scaling,
        item_delta.reshape(count_items, K * H) * scaling,
    )


def match_targets(positives, first_column, count):
    columns = first_column + jnp.arange(count, dtype=jnp.int32)
    return jnp.any(positives[:, :, None] == columns[None, None, :], axis=1).astype(jnp.float32)


def split_product(left_bf16, right_f32):
    upper = right_f32.astype(jnp.bfloat16)
    lower = (right_f32 - upper.astype(jnp.float32)).astype(jnp.bfloat16)
    dims = (((0,), (0,)), ((), ()))
    first = lax.dot_general(left_bf16, upper, dims, preferred_element_type=jnp.float32)
    second = lax.dot_general(left_bf16, lower, dims, preferred_element_type=jnp.float32)
    return first + second


def shards(
    item_features,
    tower_weight,
    gate_in,
    gate_in_bias,
    gate_out,
    gate_out_bias,
    user_table,
    user_ids,
    positive_item,
    listed_owner,
    listed_slot,
):
    block_groups = lax.axis_size("blk")
    owner_count = lax.axis_size("shard")
    group_index = lax.axis_index("blk")
    listings = listed_slot.shape[0]
    circle_part = listings * BLK
    owner_ids = listed_owner[:, 0]
    listing_order = jnp.arange(listings, dtype=jnp.int32)
    same_owner = owner_ids[:, None] == owner_ids[None, :]
    earlier = listing_order[None, :] < listing_order[:, None]
    rank_within = jnp.sum(jnp.logical_and(same_owner, earlier), axis=1)
    owner_match = owner_ids[:, None] == jnp.arange(owner_count, dtype=jnp.int32)[None, :]
    rank_match = rank_within[:, None] == jnp.arange(CAP, dtype=jnp.int32)[None, :]
    placement = jnp.logical_and(owner_match[:, :, None], rank_match[:, None, :])
    wanted = jnp.sum(jnp.where(placement, listed_slot[:, None, None] + 1, 0), axis=0) - 1
    asked_slots = lax.all_to_all(wanted, "shard", split_axis=0, concat_axis=0, tiled=True)
    slot_pick = jnp.clip(asked_slots, 0, OWN - 1).reshape(-1)
    slot_of = owner_ids * CAP + rank_within
    own_vectors = jnp.dot(item_features, tower_weight, preferred_element_type=jnp.float32).astype(
        jnp.bfloat16
    )
    own_vectors = own_vectors.reshape(OWN, BLK, E)
    outgoing = jnp.take(own_vectors, slot_pick, axis=0).reshape(owner_count, CAP, BLK, E)
    arrived = lax.all_to_all(outgoing, "shard", split_axis=0, concat_axis=0, tiled=True).reshape(
        owner_count * CAP, BLK, E
    )
    listed = jnp.take(arrived, slot_of, axis=0).reshape(circle_part, E)
    row_match = user_ids[:, None] == jnp.arange(UTAB, dtype=jnp.int32)[None, :]
    user_rows = jnp.dot(
        row_match.astype(jnp.bfloat16), user_table, preferred_element_type=jnp.float32
    ).astype(jnp.bfloat16)
    all_users = lax.all_gather(user_rows, "blk", axis=0, tiled=True)
    all_positive = lax.all_gather(positive_item, "blk", axis=0, tiled=True)
    item_delta = jnp.zeros((circle_part, E), jnp.float32)
    user_terms = []
    for source in range(block_groups):
        source_users = all_users[source * USERS : (source + 1) * USERS]
        source_positive = all_positive[source * USERS : (source + 1) * USERS]
        targets = match_targets(source_positive, group_index * circle_part, circle_part)
        user_term, item_term = pair_terms(
            source_users, listed, targets, gate_in, gate_in_bias, gate_out, gate_out_bias
        )
        user_terms.append(user_term)
        item_delta = item_delta + item_term
    user_delta = lax.psum_scatter(
        jnp.concatenate(user_terms, axis=0), "blk", scatter_dimension=0, tiled=True
    )
    listing_grads = item_delta.astype(jnp.bfloat16)
    returning = jnp.zeros((owner_count * CAP, BLK, E), jnp.bfloat16)
    returning = returning.at[slot_of].set(listing_grads.reshape(listings, BLK, E))
    returned = lax.all_to_all(
        returning.reshape(owner_count, CAP, BLK, E),
        "shard",
        split_axis=0,
        concat_axis=0,
        tiled=True,
    )
    returned = returned.reshape(owner_count * CAP, BLK * E)
    slot_hot = (
        asked_slots.reshape(-1)[None, :] == jnp.arange(OWN, dtype=jnp.int32)[:, None]
    ).astype(jnp.bfloat16)
    summed = jnp.dot(slot_hot, returned, preferred_element_type=jnp.float32).reshape(OWN * BLK, E)
    partial_value = split_product(item_features, summed)
    tower_part = lax.psum_scatter(partial_value, "shard", scatter_dimension=0, tiled=True)
    tower_gradient = lax.psum(tower_part, "blk")
    user_gradient = split_product(row_match.astype(jnp.bfloat16), user_delta)
    return (tower_gradient, user_gradient)


def solution(mesh):
    return jax.shard_map(
        shards,
        mesh=mesh,
        in_specs=(
            P("shard", None),
            P(),
            P(),
            P(),
            P(),
            P(),
            P(("blk", "shard"), None),
            P(("blk", "shard")),
            P(("blk", "shard"), None),
            P(("blk", "shard"), None),
            P(("blk", "shard")),
        ),
        out_specs=(P("shard", None), P(("blk", "shard"), None)),
        check_vma=False,
    )
```

profile of v0, /device:TPU:0, one launch (start us, length us, event | category | flops | bytes accessed | tf_op | source)
XLA Modules:
  0.0 318.4 jit_solution(14100097331826583886)
XLA Ops:
  7.2 0.9 convert_reduce_fusion
  8.1 0.7 iota_compare_fusion.7
  8.9 0.7 broadcast_add_fusion
  9.6 0.7 copy.117
  10.3 7.3 %all-to-all-start = ((s32[8,1,2]{2,1,0:T(1,128)}), s32[8,1,2]{2,1,0:T(1,128)S(1)}, u32[]{:S(2)}, u32[]{:S(2)}) async-start(s32[8,1,2]{2,1,0:T(1,128)} %copy.117), calls=%async_computation | async-start | bytes 8192 | tf_op jit(solution)/shard_map/all_to_all | solution.py:104
  17.6 9.5 %convolution_convert_fusion = bf16[4096,512]{1,0:T(8,128)(2,1)} fusion(bf16[4096,1024]{1,0:T(8,128)(2,1)} %param.11, bf16[1024,512]{1,0:T(8,128)(2,1)S(1)} %copy-done), kind=kOutput, calls=%fused_computation.8 | convolution fusion | flops 4297064448 | bytes 13631488 | tf_op jit(solution)/shard_map/dot_general | solution.py:107
  27.1 0.5 broadcast.346
  27.6 0.7 fusion.150
  28.6 2.9 gather_fusion
  31.5 1.6 broadcast_select_fusion
  33.1 6.0 %all-to-all-start.1 = ((bf16[8,2,128,512]{3,2,1,0:T(8,128)(2,1)}), bf16[8,2,128,512]{3,2,1,0:T(8,128)(2,1)S(1)}, u32[]{:S(2)}, u32[]{:S(2)}) async-start(bf16[8,2,128,512]{3,2,1,0:T(8,128)(2,1)} %broadcast_select_fusion), calls=%async_computation.1 | async-start | bytes 4194304 | tf_op jit(solution)/shard_map/all_to_all | solution.py:112
  39.4 5.2 %all-gather = bf16[4,4,512]{2,1,0:T(4,128)(2,1)S(1)} all-gather(bf16[1,4,512]{2,1,0:T(4,128)(2,1)S(1)} %fusion.65), channel_id=1, replica_groups=mesh['blk'=4,'shard'=8] {'blk'}, dimensions={0}, use_global_device_ids=true | all-gather | bytes 20480 | tf_op jit(solution)/shard_map/all_gather | solution.py:120
  44.9 5.4 %all-gather.1 = s32[4,4,16]{2,1,0:T(4,128)S(1)} all-gather(s32[1,4,16]{2,1,0:T(4,128)S(1)} %bitcast.390), channel_id=1, replica_groups=mesh['blk'=4,'shard'=8] {'blk'}, dimensions={0}, use_global_device_ids=true | all-gather | bytes 1280 | tf_op jit(solution)/shard_map/all_gather | solution.py:121
  50.5 36.3 %all-to-all-done.1 = bf16[8,2,128,512]{3,2,1,0:T(8,128)(2,1)S(1)} async-done(((bf16[8,2,128,512]{3,2,1,0:T(8,128)(2,1)}), bf16[8,2,128,512]{3,2,1,0:T(8,128)(2,1)S(1)}, u32[]{:S(2)}, u32[]{:S(2)}) %all-to-all-start.1) | async-done | bytes 2097184 | tf_op jit(solution)/shard_map/all_to_all | solution.py:112
  86.8 0.6 gather_fusion.1
  87.5 0.7 copy-done.3
  88.2 0.3 copy.120
  88.9 0.3 copy.129
  89.5 0.3 copy.133
  89.9 1.3 fusion.19
  91.2 1.6 fusion.31
  92.8 1.6 fusion.30
  94.4 1.4 fusion.20
  95.8 0.2 fusion.47
  96.0 0.3 copy.125
  96.4 0.8 fusion.29
  97.2 1.3 fusion.21
  98.7 0.3 copy.121
  99.1 0.8 fusion.28
  99.9 1.3 fusion.22
  101.6 2.2 fusion.57
  103.8 0.3 fusion.105
  104.2 1.9 fusion.86
  106.1 1.1 fusion.78
  107.3 0.8 fusion.83
  108.3 2.8 fusion.60
  111.1 2.9 fusion.59
  114.1 2.5 fusion.58
  116.5 1.3 convolution_add_fusion.4
  117.8 0.3 convolution_add_fusion.2
  118.2 0.3 fusion.40
  118.6 0.3 copy.137
  119.0 1.6 broadcast_in_dim.44
  120.5 2.5 scatter_fusion
  123.0 3.6 %all-to-all-start.2 = ((bf16[8,2,128,512]{3,2,1,0:T(8,128)(2,1)}), bf16[8,2,128,512]{3,2,1,0:T(8,128)(2,1)S(1)}, u32[]{:S(2)}, u32[]{:S(2)}) async-start(bf16[8,2,128,512]{3,2,1,0:T(8,128)(2,1)} %bitcast.47), calls=%async_computation.2 | async-start | bytes 4194304 | tf_op jit(solution)/shard_map/all_to_all | solution.py:139
  126.6 0.3 reduce-scatter.2.cloned.1.call-start
  127.0 48.1 %all-to-all-done.2 = bf16[8,2,128,512]{3,2,1,0:T(8,128)(2,1)S(1)} async-done(((bf16[8,2,128,512]{3,2,1,0:T(8,128)(2,1)}), bf16[8,2,128,512]{3,2,1,0:T(8,128)(2,1)S(1)}, u32[]{:S(2)}, u32[]{:S(2)}) %all-to-all-start.2) | async-done | bytes 2097184 | tf_op jit(solution)/shard_map/all_to_all | solution.py:139
  175.0 1.2 copy.152
  176.2 4.5 %fusion.127 = f32[32,65536]{1,0:T(8,128)} fusion(bf16[16,65536]{1,0:T(8,128)(2,1)S(1)} %bitcast.377, s32[16]{0:T(128)S(1)} %eq.130), kind=kOutput, calls=%fused_computation.181 | convolution fusion | flops 67109376 | bytes 10485824 | tf_op jit(solution)/shard_map/dot_general | solution.py:150
  180.7 7.5 %reshape.311 = f32[4096,512]{1,0:T(8,128)} reshape(f32[32,65536]{1,0:T(8,128)} %fusion.127) | data formatting | bytes 16777216 | tf_op jit(solution)/shard_map/reshape | solution.py:150
  188.1 10.8 %fusion.4 = f32[512,1024]{1,0:T(8,128)S(1)} fusion(bf16[4096,1024]{1,0:T(8,128)(2,1)} %param.11, f32[4096,512]{1,0:T(8,128)} %reshape.311), kind=kOutput, calls=%fused_computation.9 | convolution fusion | flops 4303355904 | bytes 18874368 | tf_op jit(solution)/shard_map/dot_general | solution.py:73
  198.9 9.0 %add_bitcast_fusion = f32[1024,512]{0,1:T(8,128)} fusion(f32[512,1024]{1,0:T(8,128)S(1)} %fusion.4, bf16[4096,1024]{1,0:T(8,128)(2,1)} %param.11, f32[4096,512]{1,0:T(8,128)S(1)} %copy-done.2), kind=kOutput, calls=%fused_computation.10 | convolution fusion | flops 4297588736 | bytes 20971520 | tf_op jit(solution)/shard_map/dot_general | solution.py:72
  208.0 0.6 dynamic-slice
  209.3 0.3 copy.138
  209.8 0.3 fusion.61
  210.2 0.3 fusion.62
  210.6 0.3 fusion.63
  210.9 0.3 fusion.64
  211.3 10.5 %all-reduce = f32[16,512]{1,0:T(8,128)S(1)} all-reduce(f32[16,512]{1,0:T(8,128)S(1)} %pad_maximum_fusion), channel_id=3, replica_groups=mesh['blk'=4,'shard'=8] {'blk'}, use_global_device_ids=true, to_apply=%region_17.18.clone | all-reduce | flops 8192 | bytes 65536
  221.8 0.3 fusion.129
  222.1 53.9 %reduce-scatter.2.cloned.1.call-done = f32[128,512]{0,1:T(8,128)} async-done(((f32[1024,512]{0,1:T(8,128)}), f32[128,512]{0,1:T(8,128)}) %reduce-scatter.2.cloned.1.call-update) | async-done | bytes 262160 | tf_op jit(solution)/shard_map/reduce_scatter | solution.py:152
  276.1 1.0 convolution_add_fusion.11
  277.1 32.6 %all-reduce.3.cloned.1.call-done = f32[128,512]{0,1:T(8,128)} async-done(((f32[128,512]{0,1:T(8,128)}), f32[128,512]{0,1:T(8,128)}) %all-reduce.3.cloned.1.call-update) | async-done | bytes 262160 | tf_op jit(solution)/shard_map/psum | solution.py:153
  309.8 1.8 copy.143
  (100 shorter events, 3.9 us)
Async XLA Ops:
  7.2 10.4 %copy-start = (bf16[1024,512]{1,0:T(8,128)(2,1)S(1)}, bf16[1024,512]{1,0:T(8,128)(2,1)}, u32[]{:S(2)}) copy-start(bf16[1024,512]{1,0:T(8,128)(2,1)} %param.12) | copy-start | bytes 3145732
  10.3 16.8 %all-to-all-start = ((s32[8,1,2]{2,1,0:T(1,128)}), s32[8,1,2]{2,1,0:T(1,128)S(1)}, u32[]{:S(2)}, u32[]{:S(2)}) async-start(s32[8,1,2]{2,1,0:T(1,128)} %copy.117), calls=%async_computation | async-start | bytes 8192 | tf_op jit(solution)/shard_map/all_to_all | solution.py:104
  31.4 7.7 %copy-start.22 = (bf16[128]{0:T(256)(128)(2,1)S(1)}, bf16[128]{0:T(256)(128)(2,1)}, u32[]{:S(2)}) copy-start(bf16[128]{0:T(256)(128)(2,1)} %param.14) | copy-start | bytes 772
  31.5 7.7 %copy-start.23 = (bf16[64]{0:T(256)(128)(2,1)S(1)}, bf16[64]{0:T(256)(128)(2,1)}, u32[]{:S(2)}) copy-start(bf16[64]{0:T(256)(128)(2,1)} %param.16) | copy-start | bytes 388
  31.5 7.7 %copy-start.18 = (s32[4]{0:T(128)S(1)}, s32[4]{0:T(128)}, u32[]{:S(2)}) copy-start(s32[4]{0:T(128)} %param.18) | copy-start | bytes 52
  31.5 7.7 %copy-start.20 = (bf16[128,512]{1,0:T(8,128)(2,1)S(1)}, bf16[128,512]{1,0:T(8,128)(2,1)}, u32[]{:S(2)}) copy-start(bf16[128,512]{1,0:T(8,128)(2,1)} %param.17) | copy-start | bytes 393220
  31.5 13.4 %copy-start.17 = (s32[4,16]{1,0:T(4,128)S(1)}, s32[4,16]{1,0:T(4,128)}, u32[]{:S(2)}) copy-start(s32[4,16]{1,0:T(4,128)} %param.19) | copy-start | bytes 772
  31.5 18.8 %copy-start.19 = (s32[4,1]{0,1:T(1,128)S(1)}, s32[4,1]{0,1:T(1,128)}, u32[]{:S(2)}) copy-start(s32[4,1]{0,1:T(1,128)} %param.20) | copy-start | bytes 52
  33.1 53.7 %all-to-all-start.1 = ((bf16[8,2,128,512]{3,2,1,0:T(8,128)(2,1)}), bf16[8,2,128,512]{3,2,1,0:T(8,128)(2,1)S(1)}, u32[]{:S(2)}, u32[]{:S(2)}) async-start(bf16[8,2,128,512]{3,2,1,0:T(8,128)(2,1)} %broadcast_select_fusion), calls=%async_computation.1 | async-start | bytes 4194304 | tf_op jit(solution)/shard_map/all_to_all | solution.py:112
  87.4 0.8 copy-start.3
  88.2 1.7 copy-start.11
  88.5 2.7 copy-start.21
  97.2 4.2 %copy-start.7 = (f32[4,64,512]{2,1,0:T(8,128)}, f32[4,64,512]{2,1,0:T(8,128)S(1)}, u32[]{:S(2)}) copy-start(f32[4,64,512]{2,1,0:T(8,128)S(1)} %fusion.29) | copy-start | bytes 1572868
  99.9 1.6 copy-start.9
  101.6 4.4 %copy-start.5 = (f32[4,64,512]{2,1,0:T(8,128)S(1)}, f32[4,64,512]{2,1,0:T(8,128)}, u32[]{:S(2)}) copy-start(f32[4,64,512]{2,1,0:T(8,128)} %fusion.30) | copy-start | bytes 1572868
  103.8 4.3 %copy-start.6 = (f32[4,64,512]{2,1,0:T(8,128)S(1)}, f32[4,64,512]{2,1,0:T(8,128)}, u32[]{:S(2)}) copy-start(f32[4,64,512]{2,1,0:T(8,128)} %fusion.31) | copy-start | bytes 1572868
  111.1 2.9 copy-start.8
  111.1 2.9 copy-start.10
  114.0 3.8 %copy-start.14 = (bf16[4,64,512]{2,1,0:T(8,128)(2,1)S(1)}, bf16[4,64,512]{2,1,0:T(8,128)(2,1)}, u32[]{:S(2)}) copy-start(bf16[4,64,512]{2,1,0:T(8,128)(2,1)} %fusion.59) | copy-start | bytes 786436
  114.0 4.1 %copy-start.12 = (bf16[4,64,512]{2,1,0:T(8,128)(2,1)S(1)}, bf16[4,64,512]{2,1,0:T(8,128)(2,1)}, u32[]{:S(2)}) copy-start(bf16[4,64,512]{2,1,0:T(8,128)(2,1)} %fusion.60) | copy-start | bytes 786436
  123.0 52.1 %all-to-all-start.2 = ((bf16[8,2,128,512]{3,2,1,0:T(8,128)(2,1)}), bf16[8,2,128,512]{3,2,1,0:T(8,128)(2,1)S(1)}, u32[]{:S(2)}, u32[]{:S(2)}) async-start(bf16[8,2,128,512]{3,2,1,0:T(8,128)(2,1)} %bitcast.47), calls=%async_computation.2 | async-start | bytes 4194304 | tf_op jit(solution)/shard_map/all_to_all | solution.py:139
  126.6 149.5 %reduce-scatter.2.cloned.1.call-start = ((), (), s32[]{:S(2)}) async-start(), calls=%async_computation.4 | async-start | bytes 2359296 | tf_op jit(solution)/shard_map/reduce_scatter | solution.py:152
  188.1 10.8 %copy-start.2 = (f32[4096,512]{1,0:T(8,128)S(1)}, f32[4096,512]{1,0:T(8,128)}, u32[]{:S(2)}) copy-start(f32[4096,512]{1,0:T(8,128)} %reshape.311) | copy-start | bytes 25165828
  198.9 9.1 %copy-start.24 = (u32[32]{0:T(128)S(1)}, u32[32]{0:T(128)}, u32[]{:S(2)}) copy-start(u32[32]{0:T(128)} %constant.72) | copy-start | bytes 388
  198.9 10.4 %copy-start.4 = (bf16[4,128,512]{2,1,0:T(8,128)(2,1)S(1)}, bf16[4,128,512]{2,1,0:T(8,128)(2,1)}, u32[]{:S(2)}) copy-start(bf16[4,128,512]{2,1,0:T(8,128)(2,1)} %copy-done.3) | copy-start | bytes 1572868
  207.9 1.9 copy-start.13
  207.9 2.3 copy-start.15
  207.9 2.7 copy-start.16
  207.9 101.9 %all-reduce.3.cloned.1.call-start = ((), (), s32[]{:S(2)}) async-start(), calls=%async_computation.5 | async-start | bytes 524288 | tf_op jit(solution)/shard_map/psum | solution.py:153
  209.2 102.4 %copy-start.1 = (bf16[1024,512]{1,0:T(8,128)(2,1)S(1)}, bf16[1024,512]{1,0:T(8,128)(2,1)}, u32[]{:S(2)}) copy-start(bf16[1024,512]{1,0:T(8,128)(2,1)} %param.12) | copy-start | bytes 3145732
Sparse Core Ops, SparseCore 0:
  208.0 68.0 reduce-scatter.1
  278.4 31.3 all-reduce.2
where the time goes:
time: 319 us; the launch traced here: 318 us
  waiting for transfers between devices  171 us (54%)
  matrix products  59.9 us (19%)
  local copies, waits for them, and re-layouts  24.2 us (8%)
  blocking collectives  21.1 us (7%)
  starting transfers between devices  17.2 us (5%)
  between operations  15.3 us (5%)
  other arithmetic  9.7 us (3%)
    reduce_scatter x1, waiting for transfers between devices, shards(): lax.psum_scatter(partial_value, 'shard', scatter_dimension=0, tiled=True)  53.9 us
    all_to_all x1, waiting for transfers between devices, shards(): lax.all_to_all(returning.reshape(owner_count, CAP, BLK, E), 'shard', spli...  48.1 us
    all_to_all x1, waiting for transfers between devices, shards(): lax.all_to_all(outgoing, 'shard', split_axis=0, concat_axis=0, tiled=True)  36.3 us
    psum x1, waiting for transfers between devices, shards(): tower_gradient = lax.psum(tower_part, 'blk')  32.6 us
    dot_general x2, matrix products, split_product(): lax.dot_general(left_bf16, lower, dims, preferred_element_type=jnp.float32)  11.8 us
    unnamed x1, blocking collectives  10.5 us
    dot_general x4, matrix products, pair_terms(): jnp.einsum('pg,ugi->upi', gate_in, hidden_grad, preferred_element_type=jn...  10.4 us
    dot_general x1, matrix products, shards(): jnp.dot(item_features, tower_weight, preferred_element_type=jnp.float32)  9.49 us
  transfers between devices with their start and end apart: 5, of which 4 were waited for; matrix products, arithmetic and copies ran while one was open for 4% of the time, Pallas kernels for 0%

commit v1 on v0

--- a/solution.py
+++ b/solution.py
@@ -150,7 +150,7 @@
     summed = jnp.dot(slot_hot, returned, preferred_element_type=jnp.float32).reshape(OWN * BLK, E)
     partial_value = split_product(item_features, summed)
     tower_part = lax.psum_scatter(partial_value, "shard", scatter_dimension=0, tiled=True)
-    tower_gradient = lax.psum(tower_part, "blk")
+    tower_gradient = jnp.sum(lax.all_gather(tower_part, "blk"), axis=0)
     user_gradient = split_product(row_match.astype(jnp.bfloat16), user_delta)
     return (tower_gradient, user_gradient)
 

time: 319 us -> 304 us (0.953)
  waiting for transfers between devices: 171 us -> 155 us
    psum x1 -> x0, waiting for transfers between devices: 32.6 us -> none  [shards(): tower_gradient = lax.psum(tower_part, 'blk')]
    reduce_scatter x1, waiting for transfers between devices: 53.9 us -> 66.5 us  [shards(): lax.psum_scatter(partial_value, 'shard', scatter_dimension=0, tiled=True)]
    all_gather x0 -> x1, waiting for transfers between devices: none -> 3.83 us  [shards(): tower_gradient = jnp.sum(lax.all_gather(tower_part, 'blk'), axis=0)]
  transfers between devices with their start and end apart: 5 -> 5, of which waited for: 4 -> 4; matrix products, arithmetic and copies ran while one was open for 4% -> 5% of each run, Pallas kernels for 0% -> 0%
where the time goes in v1:
time: 304 us
  waiting for transfers between devices  155 us (51%)
  matrix products  59.9 us (20%)
  local copies, waits for them, and re-layouts  24.8 us (8%)
  blocking collectives  21.3 us (7%)
  starting transfers between devices  17.2 us (6%)
  between operations  15.3 us (5%)
  other arithmetic  10.3 us (3%)
    reduce_scatter x1, waiting for transfers between devices, shards(): lax.psum_scatter(partial_value, 'shard', scatter_dimension=0, tiled=True)  66.5 us
    all_to_all x1, waiting for transfers between devices, shards(): lax.all_to_all(returning.reshape(owner_count, CAP, BLK, E), 'shard', spli...  48.1 us
    all_to_all x1, waiting for transfers between devices, shards(): lax.all_to_all(outgoing, 'shard', split_axis=0, concat_axis=0, tiled=True)  36.3 us
    dot_general x2, matrix products, split_product(): lax.dot_general(left_bf16, lower, dims, preferred_element_type=jnp.float32)  11.8 us
    unnamed x1, blocking collectives  10.8 us
    dot_general x4, matrix products, pair_terms(): jnp.einsum('pg,ugi->upi', gate_in, hidden_grad, preferred_element_type=jn...  10.4 us
    dot_general x1, matrix products, shards(): jnp.dot(item_features, tower_weight, preferred_element_type=jnp.float32)  9.49 us
    dot_general x2, matrix products, split_product(): lax.dot_general(left_bf16, upper, dims, preferred_element_type=jnp.float32)  9.26 us
  transfers between devices with their start and end apart: 5, of which 4 were waited for; matrix products, arithmetic and copies ran while one was open for 5% of the time, Pallas kernels for 0%

profile of v1, /device:TPU:0, one launch (start us, length us, event | category | flops | bytes accessed | tf_op | source)
XLA Modules:
  0.0 303.6 jit_solution(16305344721990567906)
XLA Ops:
  7.2 0.9 convert_reduce_fusion
  8.1 0.7 iota_compare_fusion.7
  8.9 0.7 broadcast_add_fusion
  9.6 0.7 copy.114
  10.3 7.3 %all-to-all-start = ((s32[8,1,2]{2,1,0:T(1,128)}), s32[8,1,2]{2,1,0:T(1,128)S(1)}, u32[]{:S(2)}, u32[]{:S(2)}) async-start(s32[8,1,2]{2,1,0:T(1,128)} %copy.114), calls=%async_computation | async-start | bytes 8192 | tf_op jit(solution)/shard_map/all_to_all | solution.py:104
  17.6 9.5 %convolution_convert_fusion = bf16[4096,512]{1,0:T(8,128)(2,1)} fusion(bf16[4096,1024]{1,0:T(8,128)(2,1)} %param.11, bf16[1024,512]{1,0:T(8,128)(2,1)S(1)} %copy-done), kind=kOutput, calls=%fused_computation.8 | convolution fusion | flops 4297064448 | bytes 13631488 | tf_op jit(solution)/shard_map/dot_general | solution.py:107
  27.1 0.5 broadcast.346
  27.6 0.7 fusion.150
  28.6 2.9 gather_fusion
  31.5 1.6 broadcast_select_fusion
  33.1 6.0 %all-to-all-start.1 = ((bf16[8,2,128,512]{3,2,1,0:T(8,128)(2,1)}), bf16[8,2,128,512]{3,2,1,0:T(8,128)(2,1)S(1)}, u32[]{:S(2)}, u32[]{:S(2)}) async-start(bf16[8,2,128,512]{3,2,1,0:T(8,128)(2,1)} %broadcast_select_fusion), calls=%async_computation.1 | async-start | bytes 4194304 | tf_op jit(solution)/shard_map/all_to_all | solution.py:112
  39.4 5.2 %all-gather.1 = bf16[4,4,512]{2,1,0:T(4,128)(2,1)S(1)} all-gather(bf16[1,4,512]{2,1,0:T(4,128)(2,1)S(1)} %fusion.65), channel_id=1, replica_groups=mesh['blk'=4,'shard'=8] {'blk'}, dimensions={0}, use_global_device_ids=true | all-gather | bytes 20480 | tf_op jit(solution)/shard_map/all_gather | solution.py:120
  44.9 5.4 %all-gather.2 = s32[4,4,16]{2,1,0:T(4,128)S(1)} all-gather(s32[1,4,16]{2,1,0:T(4,128)S(1)} %bitcast.392), channel_id=1, replica_groups=mesh['blk'=4,'shard'=8] {'blk'}, dimensions={0}, use_global_device_ids=true | all-gather | bytes 1280 | tf_op jit(solution)/shard_map/all_gather | solution.py:121
  50.5 36.3 %all-to-all-done.1 = bf16[8,2,128,512]{3,2,1,0:T(8,128)(2,1)S(1)} async-done(((bf16[8,2,128,512]{3,2,1,0:T(8,128)(2,1)}), bf16[8,2,128,512]{3,2,1,0:T(8,128)(2,1)S(1)}, u32[]{:S(2)}, u32[]{:S(2)}) %all-to-all-start.1) | async-done | bytes 2097184 | tf_op jit(solution)/shard_map/all_to_all | solution.py:112
  86.8 0.6 gather_fusion.1
  87.5 0.7 copy-done.3
  88.2 0.3 copy.117
  88.9 0.3 copy.126
  89.5 0.3 copy.130
  89.9 1.3 fusion.19
  91.2 1.6 fusion.31
  92.8 1.6 fusion.30
  94.4 1.4 fusion.20
  96.0 0.3 copy.122
  96.4 0.8 fusion.29
  97.2 1.3 fusion.21
  98.7 0.3 copy.118
  99.1 0.8 fusion.28
  99.9 1.3 fusion.22
  101.6 2.2 fusion.57
  103.8 0.3 fusion.105
  104.2 1.9 fusion.86
  106.1 1.1 fusion.78
  107.3 0.8 fusion.83
  108.3 2.8 fusion.60
  111.1 2.9 fusion.59
  114.1 2.5 fusion.58
  116.5 1.3 convolution_add_fusion.4
  117.8 0.3 convolution_add_fusion.2
  118.2 0.3 fusion.40
  118.6 0.3 copy.134
  119.0 1.6 broadcast_in_dim.44
  120.5 2.5 scatter_fusion
  123.0 3.6 %all-to-all-start.2 = ((bf16[8,2,128,512]{3,2,1,0:T(8,128)(2,1)}), bf16[8,2,128,512]{3,2,1,0:T(8,128)(2,1)S(1)}, u32[]{:S(2)}, u32[]{:S(2)}) async-start(bf16[8,2,128,512]{3,2,1,0:T(8,128)(2,1)} %bitcast.47), calls=%async_computation.2 | async-start | bytes 4194304 | tf_op jit(solution)/shard_map/all_to_all | solution.py:139
  127.0 48.1 %all-to-all-done.2 = bf16[8,2,128,512]{3,2,1,0:T(8,128)(2,1)S(1)} async-done(((bf16[8,2,128,512]{3,2,1,0:T(8,128)(2,1)}), bf16[8,2,128,512]{3,2,1,0:T(8,128)(2,1)S(1)}, u32[]{:S(2)}, u32[]{:S(2)}) %all-to-all-start.2) | async-done | bytes 2097184 | tf_op jit(solution)/shard_map/all_to_all | solution.py:139
  175.0 1.2 copy.149
  176.2 4.5 %fusion.127 = f32[32,65536]{1,0:T(8,128)} fusion(bf16[16,65536]{1,0:T(8,128)(2,1)S(1)} %bitcast.379, s32[16]{0:T(128)S(1)} %eq.130), kind=kOutput, calls=%fused_computation.181 | convolution fusion | flops 67109376 | bytes 10485824 | tf_op jit(solution)/shard_map/dot_general | solution.py:150
  180.7 7.5 %reshape.311 = f32[4096,512]{1,0:T(8,128)} reshape(f32[32,65536]{1,0:T(8,128)} %fusion.127) | data formatting | bytes 16777216 | tf_op jit(solution)/shard_map/reshape | solution.py:150
  188.1 10.8 %fusion.4 = f32[512,1024]{1,0:T(8,128)S(1)} fusion(bf16[4096,1024]{1,0:T(8,128)(2,1)} %param.11, f32[4096,512]{1,0:T(8,128)} %reshape.311), kind=kOutput, calls=%fused_computation.9 | convolution fusion | flops 4303355904 | bytes 18874368 | tf_op jit(solution)/shard_map/dot_general | solution.py:73
  198.9 9.0 %add_bitcast_fusion = f32[1024,512]{0,1:T(8,128)} fusion(f32[512,1024]{1,0:T(8,128)S(1)} %fusion.4, bf16[4096,1024]{1,0:T(8,128)(2,1)} %param.11, f32[4096,512]{1,0:T(8,128)S(1)} %copy-done.2), kind=kOutput, calls=%fused_computation.10 | convolution fusion | flops 4297588736 | bytes 20971520 | tf_op jit(solution)/shard_map/dot_general | solution.py:72
  208.0 0.6 dynamic-slice
  209.3 0.3 copy.135
  209.8 66.5 %reduce-scatter.2.cloned.1.call-done = f32[128,512]{0,1:T(8,128)} async-done(((f32[1024,512]{0,1:T(8,128)}), f32[128,512]{0,1:T(8,128)}) %reduce-scatter.2.cloned.1.call-update) | async-done | bytes 262160 | tf_op jit(solution)/shard_map/reduce_scatter | solution.py:152
  276.3 0.3 fusion.61
  276.7 0.3 fusion.62
  277.1 0.3 fusion.63
  277.4 0.3 fusion.64
  277.8 10.8 %all-reduce = f32[16,512]{1,0:T(8,128)S(1)} all-reduce(f32[16,512]{1,0:T(8,128)S(1)} %pad_maximum_fusion), channel_id=4, replica_groups=mesh['blk'=4,'shard'=8] {'blk'}, use_global_device_ids=true, to_apply=%region_17.18.clone | all-reduce | flops 8192 | bytes 65536
  288.6 0.3 fusion.129
  288.9 1.0 convolution_add_fusion.11
  289.9 3.8 %all-gather.5.cloned.1.call-done = f32[512,512]{0,1:T(8,128)} async-done(((f32[128,512]{0,1:T(8,128)}), f32[512,512]{0,1:T(8,128)}) %all-gather.5.cloned.1.call-update) | async-done | bytes 1048592 | tf_op jit(solution)/shard_map/all_gather | solution.py:153
  293.7 1.6 reshape.336
  295.3 0.6 reduce_sum.112
  295.9 0.8 copy.140
  (102 shorter events, 4.3 us)
Async XLA Ops:
  7.2 10.4 %copy-start = (bf16[1024,512]{1,0:T(8,128)(2,1)S(1)}, bf16[1024,512]{1,0:T(8,128)(2,1)}, u32[]{:S(2)}) copy-start(bf16[1024,512]{1,0:T(8,128)(2,1)} %param.12) | copy-start | bytes 3145732
  10.3 16.8 %all-to-all-start = ((s32[8,1,2]{2,1,0:T(1,128)}), s32[8,1,2]{2,1,0:T(1,128)S(1)}, u32[]{:S(2)}, u32[]{:S(2)}) async-start(s32[8,1,2]{2,1,0:T(1,128)} %copy.114), calls=%async_computation | async-start | bytes 8192 | tf_op jit(solution)/shard_map/all_to_all | solution.py:104
  31.4 7.7 %copy-start.22 = (bf16[128]{0:T(256)(128)(2,1)S(1)}, bf16[128]{0:T(256)(128)(2,1)}, u32[]{:S(2)}) copy-start(bf16[128]{0:T(256)(128)(2,1)} %param.14) | copy-start | bytes 772
  31.5 7.7 %copy-start.23 = (bf16[64]{0:T(256)(128)(2,1)S(1)}, bf16[64]{0:T(256)(128)(2,1)}, u32[]{:S(2)}) copy-start(bf16[64]{0:T(256)(128)(2,1)} %param.16) | copy-start | bytes 388
  31.5 7.7 %copy-start.18 = (s32[4]{0:T(128)S(1)}, s32[4]{0:T(128)}, u32[]{:S(2)}) copy-start(s32[4]{0:T(128)} %param.18) | copy-start | bytes 52
  31.5 7.7 %copy-start.20 = (bf16[128,512]{1,0:T(8,128)(2,1)S(1)}, bf16[128,512]{1,0:T(8,128)(2,1)}, u32[]{:S(2)}) copy-start(bf16[128,512]{1,0:T(8,128)(2,1)} %param.17) | copy-start | bytes 393220
  31.5 13.4 %copy-start.17 = (s32[4,16]{1,0:T(4,128)S(1)}, s32[4,16]{1,0:T(4,128)}, u32[]{:S(2)}) copy-start(s32[4,16]{1,0:T(4,128)} %param.19) | copy-start | bytes 772
  31.5 18.8 %copy-start.19 = (s32[4,1]{0,1:T(1,128)S(1)}, s32[4,1]{0,1:T(1,128)}, u32[]{:S(2)}) copy-start(s32[4,1]{0,1:T(1,128)} %param.20) | copy-start | bytes 52
  33.1 53.7 %all-to-all-start.1 = ((bf16[8,2,128,512]{3,2,1,0:T(8,128)(2,1)}), bf16[8,2,128,512]{3,2,1,0:T(8,128)(2,1)S(1)}, u32[]{:S(2)}, u32[]{:S(2)}) async-start(bf16[8,2,128,512]{3,2,1,0:T(8,128)(2,1)} %broadcast_select_fusion), calls=%async_computation.1 | async-start | bytes 4194304 | tf_op jit(solution)/shard_map/all_to_all | solution.py:112
  87.4 0.8 copy-start.3
  88.2 1.7 copy-start.11
  88.5 2.7 copy-start.21
  97.2 4.2 %copy-start.7 = (f32[4,64,512]{2,1,0:T(8,128)}, f32[4,64,512]{2,1,0:T(8,128)S(1)}, u32[]{:S(2)}) copy-start(f32[4,64,512]{2,1,0:T(8,128)S(1)} %fusion.29) | copy-start | bytes 1572868
  99.9 1.6 copy-start.9
  101.6 4.4 %copy-start.5 = (f32[4,64,512]{2,1,0:T(8,128)S(1)}, f32[4,64,512]{2,1,0:T(8,128)}, u32[]{:S(2)}) copy-start(f32[4,64,512]{2,1,0:T(8,128)} %fusion.30) | copy-start | bytes 1572868
  103.8 4.3 %copy-start.6 = (f32[4,64,512]{2,1,0:T(8,128)S(1)}, f32[4,64,512]{2,1,0:T(8,128)}, u32[]{:S(2)}) copy-start(f32[4,64,512]{2,1,0:T(8,128)} %fusion.31) | copy-start | bytes 1572868
  111.1 2.9 copy-start.8
  111.1 2.9 copy-start.10
  114.0 3.8 %copy-start.14 = (bf16[4,64,512]{2,1,0:T(8,128)(2,1)S(1)}, bf16[4,64,512]{2,1,0:T(8,128)(2,1)}, u32[]{:S(2)}) copy-start(bf16[4,64,512]{2,1,0:T(8,128)(2,1)} %fusion.59) | copy-start | bytes 786436
  114.0 4.1 %copy-start.12 = (bf16[4,64,512]{2,1,0:T(8,128)(2,1)S(1)}, bf16[4,64,512]{2,1,0:T(8,128)(2,1)}, u32[]{:S(2)}) copy-start(bf16[4,64,512]{2,1,0:T(8,128)(2,1)} %fusion.60) | copy-start | bytes 786436
  123.0 52.1 %all-to-all-start.2 = ((bf16[8,2,128,512]{3,2,1,0:T(8,128)(2,1)}), bf16[8,2,128,512]{3,2,1,0:T(8,128)(2,1)S(1)}, u32[]{:S(2)}, u32[]{:S(2)}) async-start(bf16[8,2,128,512]{3,2,1,0:T(8,128)(2,1)} %bitcast.47), calls=%async_computation.2 | async-start | bytes 4194304 | tf_op jit(solution)/shard_map/all_to_all | solution.py:139
  126.6 149.7 %reduce-scatter.2.cloned.1.call-start = ((), (), s32[]{:S(2)}) async-start(), calls=%async_computation.4 | async-start | bytes 2359296 | tf_op jit(solution)/shard_map/reduce_scatter | solution.py:152
  188.1 10.8 %copy-start.2 = (f32[4096,512]{1,0:T(8,128)S(1)}, f32[4096,512]{1,0:T(8,128)}, u32[]{:S(2)}) copy-start(f32[4096,512]{1,0:T(8,128)} %reshape.311) | copy-start | bytes 25165828
  198.9 9.1 %copy-start.24 = (u32[32]{0:T(128)S(1)}, u32[32]{0:T(128)}, u32[]{:S(2)}) copy-start(u32[32]{0:T(128)} %constant.72) | copy-start | bytes 388
  198.9 10.4 %copy-start.4 = (bf16[4,128,512]{2,1,0:T(8,128)(2,1)S(1)}, bf16[4,128,512]{2,1,0:T(8,128)(2,1)}, u32[]{:S(2)}) copy-start(bf16[4,128,512]{2,1,0:T(8,128)(2,1)} %copy-done.3) | copy-start | bytes 1572868
  207.9 68.4 %copy-start.13 = (bf16[4,64,512]{2,1,0:T(8,128)(2,1)S(1)}, bf16[4,64,512]{2,1,0:T(8,128)(2,1)}, u32[]{:S(2)}) copy-start(bf16[4,64,512]{2,1,0:T(8,128)(2,1)} %fusion.60) | copy-start | bytes 786436
  207.9 68.8 %copy-start.15 = (bf16[4,64,512]{2,1,0:T(8,128)(2,1)S(1)}, bf16[4,64,512]{2,1,0:T(8,128)(2,1)}, u32[]{:S(2)}) copy-start(bf16[4,64,512]{2,1,0:T(8,128)(2,1)} %fusion.59) | copy-start | bytes 786436
  207.9 69.2 %copy-start.16 = (bf16[4,64,512]{2,1,0:T(8,128)(2,1)S(1)}, bf16[4,64,512]{2,1,0:T(8,128)(2,1)}, u32[]{:S(2)}) copy-start(bf16[4,64,512]{2,1,0:T(8,128)(2,1)} %fusion.58) | copy-start | bytes 786436
  207.9 85.8 %all-gather.5.cloned.1.call-start = ((), (), s32[]{:S(2)}) async-start(), calls=%async_computation.5 | async-start | bytes 1310720 | tf_op jit(solution)/shard_map/all_gather | solution.py:153
  276.6 20.2 %copy-start.1 = (bf16[1024,512]{1,0:T(8,128)(2,1)S(1)}, bf16[1024,512]{1,0:T(8,128)(2,1)}, u32[]{:S(2)}) copy-start(bf16[1024,512]{1,0:T(8,128)(2,1)} %param.12) | copy-start | bytes 3145732
Sparse Core Ops, SparseCore 0:
  208.0 68.2 reduce-scatter.1
  277.8 15.8 all-gather.4
